TPU v7x, 32 devices: a whole 2x2x4 slice. The times are simulated.
32 devices in a mesh: prow: 16 (over z, y, x), pcol: 2 (over core).
Axes of the slice: x: 2, y: 2, z: 4, core: 2. Of those that a mesh axis runs over, the one named last changes fastest.
Arguments:
- right_sides: float32 [32, 1, 4096], P(None, None, 'prow'), may hold values from -6 to 6
- factor: bfloat16 [1, 4096, 8, 512], P(None, 'prow', None, 'pcol'), as said below
- node_sizes: int32 [7], replicated, may hold values from 1 to 9, 16 in all
- row_blocks: int32 [7, 16], replicated, may hold values 0 or 1
Outputs:
- forward: float32 [32, 1, 4096], P(None, None, 'prow')
- solution: float32 [32, 8, 512], P(None, None, 'pcol')
Inputs may be any that keep to these rules, and one draw needn't show every extreme that they name: factor is zero above its diagonal; its diagonal lies between 0.5 and 1. `row_blocks`: flags of tiles that belong to no proper ancestor of the supernode are ignored.
All inputs are finite; a program needn't handle non-finite values.
Results may differ from a plain program's by a relative error of at most 0.0047.
Values may be sent and summed in bfloat16 or wider, within the bound.
A program may use at most 64 MiB of HBM per device.

v0:
```python
import functools

import jax
import jax.numpy as jnp
from jax import lax
from jax.experimental import pallas as pl
from jax.experimental.pallas import tpu as pltpu
from jax.sharding import PartitionSpec as P

MESH = pl.DeviceIdType.MESH
NT_DIMS = (((1,), (1,)), ((), ()))
GROUP = 2
SPLIT = 8
CHUNK = 64
LANES = 128
NN_DIMS = (((1,), (0,)), ((), ()))


def kernel(
    R, C, CT, LEVELS,
    sizes_ref, blocks_ref, b_ref, factor_ref,
    fwd_ref, sol_ref,
    raw, wide, a_ref,
    ag_src, ag_buf, comb_buf, rs_src, rs_buf, share_buf, fin_src, fin_buf, update,
    ag_send, ag_recv, comb_send, comb_recv, rs_send, rs_recv,
    share_send, share_recv, fin_send, fin_recv, load_sem,
):
    SN = sizes_ref.shape[0]
    me = lax.axis_index("prow")
    col = lax.axis_index("pcol")
    mine = lax.rem(me, C) == col
    slot = me // C
    before = (me + C - 1 - col) // C
    T = b_ref.shape[2]

    load = pltpu.make_async_copy(factor_ref.at[0], raw, load_sem)
    load.start()
    barrier = pltpu.get_barrier_semaphore()

    def greet_row(step, carry):
        pl.semaphore_signal(
            barrier, inc=1, device_id=(lax.rem(me + step, R), col), device_id_type=MESH
        )
        return carry

    def greet_col(step, carry):
        pl.semaphore_signal(
            barrier, inc=1, device_id=(me, lax.rem(col + step, C)), device_id_type=MESH
        )
        return carry

    lax.fori_loop(1, R, greet_row, 0)
    lax.fori_loop(1, C, greet_col, 0)

    ends = []
    total = jnp.int32(0)
    for s in range(SN):
        total = total + sizes_ref[s]
        ends.append(total)

    def node_of(tile):
        count = jnp.int32(0)
        for s in range(SN):
            count = count + jnp.where(ends[s] <= tile, 1, 0)
        return jnp.minimum(count, SN - 1)

    row_node = node_of(me)
    row_label = SN - row_node
    row_level = jnp.int32(0)
    for e in range(1, LEVELS):
        row_level = row_level + jnp.where(row_label >= 2**e, 1, 0)
    same, linked = [], []
    for s in range(CT):
        node = node_of(s * C + col)
        label = SN - node
        above = jnp.int32(0)
        for gap in range(1, LEVELS):
            above = above + jnp.where(jnp.right_shift(label, gap) == row_label, 1, 0)
        flag = jnp.where(blocks_ref[node, me] == 1, 1, 0)
        low = jnp.where(s * C + col <= me, 1, 0)
        same.append(jnp.where(node == row_node, 1, 0) * low > 0)
        linked.append(above * flag * low > 0)

    b = b_ref[:, 0, :]
    pl.semaphore_wait(barrier, R - 1 + C - 1)

    def relayout(step, carry):
        start = pl.multiple_of(step * CHUNK, CHUNK)
        rows = pl.ds(start, CHUNK)
        for h in range(T // LANES):
            block = raw[rows, :, h * LANES:(h + 1) * LANES].astype(jnp.float32)
            wide[h] = block.reshape(CHUNK * CT, LANES)
        for s in range(CT):
            for h in range(T // LANES):
                part = wide[h, pl.ds(s, CHUNK, stride=CT), :]
                at = s * T + h * LANES
                a_ref[rows, at:at + LANES] = part.astype(jnp.bfloat16)
        return carry

    def ag_copy(rnd, k):
        return pltpu.make_async_remote_copy(
            src_ref=ag_src.at[rnd], dst_ref=ag_buf.at[rnd, slot],
            send_sem=ag_send.at[k], recv_sem=ag_recv.at[rnd, slot],
            device_id=(k, col), device_id_type=MESH,
        )

    def send_row(rnd, value):
        @pl.when(mine)
        def _():
            if rnd > 0:
                lax.fori_loop(
                    me + 1, R, lambda k, x: (ag_copy(rnd, k).wait_send(), x)[1], 0
                )
            ag_src[rnd] = value
            lax.fori_loop(
                me + 1, R, lambda k, x: (ag_copy(rnd, k).start(), x)[1], 0
            )
            ag_buf[rnd, slot] = value

    def arrive_at(rnd, s):
        pltpu.make_async_remote_copy(
            src_ref=ag_src.at[rnd], dst_ref=ag_buf.at[rnd, s],
            send_sem=ag_send.at[0], recv_sem=ag_recv.at[rnd, s],
            device_id=(me, col), device_id_type=MESH,
        ).wait_recv()

    def multiply(rnd, masks):
        zero = jnp.zeros((b.shape[0], T), jnp.bfloat16)
        out = None
        for last in range(CT, 0, -GROUP):
            group = range(max(last - GROUP, 0), last)
            for s in reversed(group):
                pl.when(s < before)(functools.partial(arrive_at, rnd, s))
            parts = [jnp.where(masks[s], ag_buf[rnd, s], zero) for s in group]
            value = lax.dot_general(
                jnp.concatenate(parts, axis=1), a_ref[:, group[0] * T:last * T], NT_DIMS,
                preferred_element_type=jnp.float32,
            )
            out = value if out is None else out + value
        return out

    def comb_copy(rnd, step):
        to = lax.rem(col + step, C)
        return pltpu.make_async_remote_copy(
            src_ref=comb_buf.at[rnd, col], dst_ref=comb_buf.at[rnd, col],
            send_sem=comb_send.at[rnd, step], recv_sem=comb_recv.at[rnd, col],
            device_id=(me, to), device_id_type=MESH,
        )

    def combine(rnd, partial):
        comb_buf[rnd, col] = partial
        for step in range(1, C):
            comb_copy(rnd, step).start()
        for step in range(1, C):
            origin = lax.rem(col + step, C)
            pltpu.make_async_remote_copy(
                src_ref=comb_buf.at[rnd, col], dst_ref=comb_buf.at[rnd, origin],
                send_sem=comb_send.at[rnd, step], recv_sem=comb_recv.at[rnd, origin],
                device_id=(me, origin), device_id_type=MESH,
            ).wait_recv()
        out = comb_buf[rnd, 0]
        for c in range(1, C):
            out = out + comb_buf[rnd, c]
        return out

    zeros = jnp.zeros(b.shape, jnp.float32)
    forward = zeros
    correction = zeros
    rnd = 0
    for level in range(LEVELS - 1, -1, -1):
        here = row_level == level
        send_row(rnd, (b - correction).astype(jnp.bfloat16))
        if rnd == 0:
            load.wait()
            lax.fori_loop(0, T // CHUNK, relayout, 0)
        solved = combine(rnd, multiply(rnd, same))
        solved = jnp.where(here, solved, zeros)
        forward = forward + solved
        rnd += 1
        if level > 0:
            send_row(rnd, solved.astype(jnp.bfloat16))
            correction = correction + combine(rnd, multiply(rnd, linked))
            rnd += 1
    fwd_ref[...] = forward
    rounded = forward.astype(jnp.bfloat16)
    base = rounded.astype(jnp.float32)

    def rs_copy(rnd, s):
        return pltpu.make_async_remote_copy(
            src_ref=rs_src.at[rnd, s], dst_ref=rs_buf.at[rnd, me],
            send_sem=rs_send.at[rnd, s], recv_sem=rs_recv.at[rnd, me],
            device_id=(s * C + col, col), device_id_type=MESH,
        )

    def scatter(rnd, value, masks):
        for last in range(CT, 0, -SPLIT):
            first = max(last - SPLIT, 0)
            blocks = lax.dot_general(
                value, a_ref[:, first * T:last * T], NN_DIMS,
                preferred_element_type=jnp.float32,
            )
            for s in reversed(range(first, last)):
                rs_src[rnd, s] = jnp.where(
                    masks[s], blocks[:, (s - first) * T:(s - first + 1) * T], zeros
                ).astype(jnp.bfloat16)
                pl.when(s < before)(rs_copy(rnd, s).start)

    def reduce(rnd):
        def arrive(k, carry):
            pltpu.make_async_remote_copy(
                src_ref=rs_src.at[rnd, 0], dst_ref=rs_buf.at[rnd, k],
                send_sem=rs_send.at[rnd, 0], recv_sem=rs_recv.at[rnd, k],
                device_id=(k, col), device_id_type=MESH,
            ).wait_recv()
            return carry + rs_buf[rnd, k].astype(jnp.float32)

        return lax.fori_loop(me + 1, R, arrive, rs_src[rnd, slot].astype(jnp.float32))

    def share_copy(rnd, step):
        return pltpu.make_async_remote_copy(
            src_ref=share_buf.at[rnd], dst_ref=share_buf.at[rnd],
            send_sem=share_send.at[rnd, step], recv_sem=share_recv.at[rnd],
            device_id=(me, lax.rem(col + step, C)), device_id_type=MESH,
        )

    def share(rnd, finish):
        @pl.when(mine)
        def _():
            share_buf[rnd] = finish(reduce(rnd)).astype(jnp.bfloat16)
            for step in range(1, C):
                share_copy(rnd, step).start()

        if C > 1:
            @pl.when(jnp.logical_not(mine))
            def _():
                share_copy(rnd, 1).wait_recv()

        return share_buf[rnd]

    fin_src[...] = zeros
    update[...] = zeros
    rnd = 0
    current = jnp.where(row_level == 0, rounded, jnp.zeros_like(rounded))
    for level in range(LEVELS - 1):
        scatter(rnd, current, same)

        def keep(value):
            fin_src[...] = fin_src[...] + value
            return value

        solved = share(rnd, keep)
        rnd += 1
        scatter(rnd, solved, linked)

        def settle(value):
            update[...] = update[...] + value
            return jnp.where(row_level == level + 1, base - update[...], zeros)

        current = share(rnd, settle)
        rnd += 1
    scatter(rnd, current, same)

    def fin_copy(step):
        return pltpu.make_async_remote_copy(
            src_ref=fin_buf.at[slot], dst_ref=fin_buf.at[slot],
            send_sem=fin_send.at[step], recv_sem=fin_recv.at[slot],
            device_id=(lax.rem(me + step, R), col), device_id_type=MESH,
        )

    @pl.when(mine)
    def _():
        fin_buf[slot] = (fin_src[...] + reduce(rnd)).astype(jnp.bfloat16)
        lax.fori_loop(1, R, lambda step, x: (fin_copy(step).start(), x)[1], 0)

    def fin_arrive(s, carry):
        @pl.when(s * C + col != me)
        def _():
            pltpu.make_async_remote_copy(
                src_ref=fin_buf.at[s], dst_ref=fin_buf.at[s],
                send_sem=fin_send.at[0], recv_sem=fin_recv.at[s],
                device_id=(me, col), device_id_type=MESH,
            ).wait_recv()
        return carry

    for r in range(comb_buf.shape[0]):
        for step in range(1, C):
            comb_copy(r, step).wait_send()
    for r in range(rs_buf.shape[0]):
        lax.fori_loop(0, before, lambda s, x: (rs_copy(r, s).wait_send(), x)[1], 0)

    @pl.when(mine)
    def _():
        lax.fori_loop(me + 1, R, lambda k, x: (ag_copy(0, k).wait_send(), x)[1], 0)
        for r in range(share_buf.shape[0]):
            for step in range(1, C):
                share_copy(r, step).wait_send()

    lax.fori_loop(0, CT, fin_arrive, 0)
    for s in range(CT):
        sol_ref[s] = fin_buf[s]

    @pl.when(mine)
    def _():
        lax.fori_loop(1, R, lambda step, x: (fin_copy(step).wait_send(), x)[1], 0)


def finish_kernel(rows_ref, tiles_ref, fwd_ref, sol_ref):
    fwd_ref[:, 0, :] = rows_ref[...]
    for s in range(tiles_ref.shape[0]):
        sol_ref[:, s, :] = tiles_ref[s].astype(jnp.float32)


def shards(R, C, right_sides, factor, node_sizes, row_blocks):
    rhs, row_tiles, T = right_sides.shape
    rows, CT = factor.shape[1], factor.shape[2]
    levels = (node_sizes.shape[0] + 1).bit_length() - 1
    assert row_tiles == 1 and rows == T and CT * C == R
    rounds = 2 * levels - 1
    vmem = pl.BlockSpec(memory_space=pltpu.VMEM)
    smem = pl.BlockSpec(memory_space=pltpu.SMEM)
    dma = pltpu.SemaphoreType.DMA
    bf16, f32 = jnp.bfloat16, jnp.float32
    forward, tiles = pl.pallas_call(
        functools.partial(kernel, R, C, CT, levels),
        out_shape=(
            jax.ShapeDtypeStruct((rhs, T), f32),
            jax.ShapeDtypeStruct((CT, rhs, T), bf16),
        ),
        in_specs=[smem, smem, vmem, pl.BlockSpec(memory_space=pl.ANY)],
        out_specs=(vmem, vmem),
        scratch_shapes=[
            pltpu.VMEM((rows, CT, T), bf16),
            pltpu.VMEM((T // LANES, CHUNK * CT, LANES), f32),
            pltpu.VMEM((rows, CT * T), bf16),
            pltpu.VMEM((rounds, rhs, T), bf16),
            pltpu.VMEM((rounds, CT, rhs, T), bf16),
            pltpu.VMEM((rounds, C, rhs, T), f32),
            pltpu.VMEM((rounds, CT, rhs, T), bf16),
            pltpu.VMEM((rounds, R, rhs, T), bf16),
            pltpu.VMEM((rounds - 1, rhs, T), bf16),
            pltpu.VMEM((rhs, T), f32),
            pltpu.VMEM((CT, rhs, T), bf16),
            pltpu.VMEM((rhs, T), f32),
            dma((R,)),
            dma((rounds, CT)),
            dma((rounds, C)),
            dma((rounds, C)),
            dma((rounds, CT)),
            dma((rounds, R)),
            dma((rounds - 1, C)),
            dma((rounds - 1,)),
            dma((R,)),
            dma((CT,)),
            dma,
        ],
        compiler_params=pltpu.CompilerParams(collective_id=0, has_side_effects=True),
        name="tree_solve",
    )(node_sizes, row_blocks, right_sides, factor)

    return pl.pallas_call(
        finish_kernel,
        out_shape=(
            jax.ShapeDtypeStruct((rhs, 1, T), f32),
            jax.ShapeDtypeStruct((rhs, CT, T), f32),
        ),
        in_specs=[vmem, vmem],
        out_specs=(vmem, vmem),
        name="place",
    )(forward, tiles)


def solution(mesh):
    in_specs = (P(None, None, "prow"), P(None, "prow", None, "pcol"), P(), P())
    out_specs = (P(None, None, "prow"), P(None, None, "pcol"))
    body = functools.partial(shards, mesh.shape["prow"], mesh.shape["pcol"])
    return jax.shard_map(
        body, mesh=mesh, in_specs=in_specs, out_specs=out_specs, check_vma=False
    )
```

profile of v0, /device:TPU:0, one launch (start us, length us, event | category | flops | bytes accessed | tf_op | source)
XLA Modules:
  0.0 66.6 jit_solution(8898816475294856831)
XLA Ops:
  0.6 64.3 %tree_solve.1 = (f32[32,256]{1,0:T(8,128)}, bf16[8,32,256]{2,1,0:T(8,128)(2,1)}) custom-call(s32[7]{0:T(128)} %sizes_ref.1, s32[7,16]{1,0:T(8,128)} %blocks_ref.1, f32[32,1,256]{2,1,0:T(1,128)} %b_ref.1, bf16[1,256,8,256]{3,2,1,0:T(8,128)(2,1)} %factor_ref.1), custom_call_target="tpu_custom_call" | custom-call | tf_op jit(solution)/shard_map/tree_solve/pallas_call | solution.py:323
  64.9 1.7 %place.1 = (f32[32,1,256]{2,1,0:T(1,128)}, f32[32,8,256]{2,1,0:T(8,128)}) custom-call(f32[32,256]{1,0:T(8,128)} %get-tuple-element.4.rows_ref, bf16[8,32,256]{2,1,0:T(8,128)(2,1)} %get-tuple-element.5.tiles_ref), custom_call_target="tpu_custom_call" | custom-call | tf_op jit(solution)/shard_map/place/pallas_call | solution.py:360
where the time goes:
time: 66.8 us; the launch traced here: 66.6 us
  Pallas kernels  66 us (99%)
    pallas_call x1, Pallas kernels, shards(): pl.pallas_call(functools.partial(kernel, R, C, CT, levels), out_shape=(ja...  64.3 us
    pallas_call x1, Pallas kernels, shards(): pl.pallas_call(finish_kernel, out_shape=(jax.ShapeDtypeStruct((rhs, 1, T)...  1.72 us

commit v1 on v0

v1 whole, which is shorter than its diff:
```python
import functools

import jax
import jax.numpy as jnp
from jax import lax
from jax.experimental import pallas as pl
from jax.experimental.pallas import tpu as pltpu
from jax.sharding import PartitionSpec as P

MESH = pl.DeviceIdType.MESH
NT_DIMS = (((1,), (1,)), ((), ()))
NN_DIMS = (((1,), (0,)), ((), ()))
GATHER = 2
SPLIT = 2
CHUNK = 64
LANES = 128
PACK = 16


def kernel(
    R, C, CT, LEVELS, H,
    sizes_ref, blocks_ref, b_ref, factor_ref,
    fwd_ref, sol_ref,
    raw, wide, a_ref,
    ag_src, ag_buf, rs_src, rs_buf, fwd_buf, fin_src, fin_buf,
    ag_send, ag_recv, rs_send, rs_recv,
    fwd_send, fwd_recv, fin_send, fin_recv, raw_send, raw_recv, load_sem,
):
    SN = sizes_ref.shape[0]
    me = lax.axis_index("prow")
    col = lax.axis_index("pcol")
    base = (col // H) * H
    g = lax.rem(col, H)
    T = b_ref.shape[2]
    Q = b_ref.shape[0] // H
    f32, bf16 = jnp.float32, jnp.bfloat16

    widest = R - SN + 1
    lows, highs = [], []
    for level in range(LEVELS):
        first = SN - 1 - (2 ** (level + 1) - 2)
        last = SN - 1 - (2**level - 1)
        lows.append(first)
        highs.append(R - SN + last)

    load = pltpu.make_async_copy(factor_ref.at[0], raw.at[col], load_sem)
    load.start()
    barrier = pltpu.get_barrier_semaphore()

    def greet(step, carry):
        row = lax.rem(me + R - 1 - step, R)
        for j in range(H):
            @pl.when(jnp.logical_or(step < R - 1, j > 0))
            def _():
                pl.semaphore_signal(
                    barrier, inc=1, device_id=(row, base + lax.rem(g + j, H)),
                    device_id_type=MESH,
                )
        return carry

    lax.fori_loop(0, R, greet, 0)

    def greet_row(step, carry):
        pl.semaphore_signal(
            barrier, inc=1, device_id=(me, lax.rem(base + H + step, C)),
            device_id_type=MESH,
        )
        return carry

    lax.fori_loop(0, C - H, greet_row, 0)

    ends = []
    total = jnp.int32(0)
    for s in range(SN):
        total = total + sizes_ref[s]
        ends.append(total)

    def node_of(tile):
        count = jnp.int32(0)
        for s in range(SN):
            count = count + jnp.where(ends[s] <= tile, 1, 0)
        return jnp.minimum(count, SN - 1)

    def level_of(label):
        level = jnp.int32(0)
        for e in range(1, LEVELS):
            level = level + jnp.where(label >= 2**e, 1, 0)
        return level

    row_node = node_of(me)
    row_label = SN - row_node
    row_level = level_of(row_label)
    same, linked, tile_level = [], [], []
    for k in range(R):
        node = node_of(k)
        label = SN - node
        above = jnp.int32(0)
        for gap in range(1, LEVELS):
            above = above + jnp.where(jnp.right_shift(label, gap) == row_label, 1, 0)
        flag = jnp.where(blocks_ref[node, me] == 1, 1, 0)
        low = jnp.where(k <= me, 1, 0)
        same.append(jnp.where(node == row_node, 1, 0) * low)
        linked.append(above * flag * low)
        tile_level.append(level_of(label))

    def inner(level):
        here = jnp.where(row_level == level, 1, 0)
        return [same[k] * here > 0 for k in range(R)]

    def outer(level):
        return [
            linked[k] * jnp.where(tile_level[k] == level, 1, 0) > 0 for k in range(R)
        ]

    b = b_ref[pl.ds(pl.multiple_of(g * Q, Q), Q), 0, :]
    zeros = jnp.zeros((Q, T), f32)

    def relayout(c):
        def body(step, carry):
            start = pl.multiple_of(step * CHUNK, CHUNK)
            rows = pl.ds(start, CHUNK)
            for h in range(T // LANES):
                block = raw[c, rows, :, h * LANES:(h + 1) * LANES].astype(f32)
                wide[h] = block.reshape(CHUNK * CT, LANES)
            for s in range(CT):
                for h in range(T // LANES):
                    part = wide[h, pl.ds(s, CHUNK, stride=CT), :]
                    at = pl.multiple_of((s * C + c) * T + h * LANES, LANES)
                    a_ref[rows, pl.ds(at, LANES)] = part.astype(bf16)
            return carry

        lax.fori_loop(0, T // CHUNK, body, 0)

    load.wait()
    relayout(col)
    pl.semaphore_wait(barrier, R * H - 1 + C - H)

    def raw_copy(step):
        return pltpu.make_async_remote_copy(
            src_ref=factor_ref.at[0], dst_ref=raw.at[col],
            send_sem=raw_send.at[step], recv_sem=raw_recv.at[col],
            device_id=(me, lax.rem(col + step, C)), device_id_type=MESH,
        )

    def raw_arrive(step, carry):
        origin = lax.rem(col + step, C)
        pltpu.make_async_remote_copy(
            src_ref=factor_ref.at[0], dst_ref=raw.at[origin],
            send_sem=raw_send.at[step], recv_sem=raw_recv.at[origin],
            device_id=(me, origin), device_id_type=MESH,
        ).wait_recv()
        relayout(origin)
        return carry

    def ag_copy(rnd, k):
        return pltpu.make_async_remote_copy(
            src_ref=ag_src.at[rnd], dst_ref=ag_buf.at[rnd, me],
            send_sem=ag_send.at[rnd, k], recv_sem=ag_recv.at[rnd, me],
            device_id=(k, col), device_id_type=MESH,
        )

    def forward_range(level, far):
        if far:
            first, last, reach = lows[level - 1], R - 1, R
        else:
            first, last, reach = lows[level], highs[level], widest - 1
        active = jnp.logical_and(me >= lows[level], me <= highs[level])
        start = jnp.maximum(me + 1, first)
        stop = jnp.minimum(me + reach, last) + 1
        return start, jnp.where(active, jnp.maximum(stop, start), start)

    def send_row(rnd, level, far, value):
        start, stop = forward_range(level, far)
        ag_src[rnd] = value
        lax.fori_loop(
            0, stop - start, lambda i, x: (ag_copy(rnd, stop - 1 - i).start(), x)[1], 0
        )
        ag_buf[rnd, me] = value

    def sent_row(rnd, level, far):
        start, stop = forward_range(level, far)
        lax.fori_loop(start, stop, lambda k, x: (ag_copy(rnd, k).wait_send(), x)[1], 0)

    def row_arrive(rnd, k):
        pltpu.make_async_remote_copy(
            src_ref=ag_src.at[rnd], dst_ref=ag_buf.at[rnd, k],
            send_sem=ag_send.at[rnd, k], recv_sem=ag_recv.at[rnd, k],
            device_id=(me, col), device_id_type=MESH,
        ).wait_recv()

    def multiply(rnd, level, far, masks):
        lo, hi = lows[level], highs[level]
        zero = jnp.zeros((Q, T), bf16)
        out = None
        for last in range(hi + 1, lo, -GATHER):
            group = range(max(last - GATHER, lo), last)
            for k in reversed(group):
                if far:
                    due = jnp.logical_and(me > k, me >= lows[level - 1])
                else:
                    due = jnp.logical_and(me > k, me <= min(hi, k + widest - 1))
                pl.when(due)(functools.partial(row_arrive, rnd, k))
            parts = [jnp.where(masks[k], ag_buf[rnd, k], zero) for k in group]
            value = lax.dot_general(
                jnp.concatenate(parts, axis=1), a_ref[:, group[0] * T:last * T], NT_DIMS,
                preferred_element_type=f32,
            )
            out = value if out is None else out + value
        return out

    forward = zeros
    correction = zeros
    rnd = 0
    before = None
    for level in range(LEVELS - 1, -1, -1):
        send_row(rnd, level, False, (b - correction).astype(bf16))
        if rnd == 0:
            for step in range(1, C):
                raw_copy(step).start()
            lax.fori_loop(1, C, raw_arrive, 0)
        if before is not None:
            sent_row(*before)
        before = (rnd, level, False)
        solved = multiply(rnd, level, False, inner(level))
        solved = jnp.where(row_level == level, solved, zeros)
        forward = forward + solved
        rnd += 1
        if level > 0:
            send_row(rnd, level, True, solved.astype(bf16))
            sent_row(*before)
            before = (rnd, level, True)
            correction = correction + multiply(rnd, level, True, outer(level))
            rnd += 1
    rounded = forward.astype(bf16)
    start_value = rounded.astype(f32)

    def rs_copy(rnd, t):
        return pltpu.make_async_remote_copy(
            src_ref=rs_src.at[rnd, t], dst_ref=rs_buf.at[rnd, me],
            send_sem=rs_send.at[rnd, t], recv_sem=rs_recv.at[rnd, me],
            device_id=(t, col), device_id_type=MESH,
        )

    def goes(level, far, t):
        if far:
            return jnp.logical_and(me > t, me >= lows[level - 1])
        return jnp.logical_and(me > t, me <= min(highs[level], t + widest - 1))

    def scatter(rnd, level, far, value, masks):
        lo, hi = lows[level], highs[level]
        for first in range(lo, hi + 1, SPLIT):
            group = range(first, min(first + SPLIT, hi + 1))
            blocks = lax.dot_general(
                value, a_ref[:, group[0] * T:(group[-1] + 1) * T], NN_DIMS,
                preferred_element_type=f32,
            )
            for i, t in enumerate(group):
                rs_src[rnd, t] = jnp.where(
                    masks[t], blocks[:, i * T:(i + 1) * T], zeros
                ).astype(bf16)
                pl.when(goes(level, far, t))(rs_copy(rnd, t).start)

    def scattered(rnd, level, far):
        for t in range(lows[level], highs[level] + 1):
            pl.when(goes(level, far, t))(rs_copy(rnd, t).wait_send)

    def reduce(rnd, level, far, out):
        def arrive(k, carry):
            pltpu.make_async_remote_copy(
                src_ref=rs_src.at[rnd, 0], dst_ref=rs_buf.at[rnd, k],
                send_sem=rs_send.at[rnd, 0], recv_sem=rs_recv.at[rnd, k],
                device_id=(k, col), device_id_type=MESH,
            ).wait_recv()
            return carry + rs_buf[rnd, k].astype(f32)

        active = jnp.logical_and(me >= lows[level], me <= highs[level])
        if far:
            start, last = jnp.maximum(me + 1, lows[level - 1]), jnp.int32(R - 1)
        else:
            start = me + 1
            last = jnp.minimum(me + widest - 1, highs[level])
        stop = jnp.where(active, jnp.maximum(last + 1, start), start)
        return lax.fori_loop(start, stop, arrive, out)

    def fin_copy(row):
        return pltpu.make_async_remote_copy(
            src_ref=fin_src, dst_ref=fin_buf.at[me // C, g],
            send_sem=fin_send.at[row], recv_sem=fin_recv.at[me // C, g],
            device_id=(row, lax.rem(me, C)), device_id_type=MESH,
        )

    giver = lax.rem(me, C) // H == col // H
    local = lax.rem(me, C) == col

    def give(value):
        fin_src[...] = value.astype(bf16)

        def one(step, carry):
            fin_copy(lax.rem(me + step, R)).start()
            return carry

        lax.fori_loop(1, R, one, 0)

        @pl.when(local)
        def _():
            fin_buf[me // C, g] = value.astype(bf16)

        @pl.when(jnp.logical_not(local))
        def _():
            fin_copy(me).start()

    def fwd_copy(j):
        return pltpu.make_async_remote_copy(
            src_ref=fwd_buf.at[g], dst_ref=fwd_buf.at[g],
            send_sem=fwd_send.at[j], recv_sem=fwd_recv.at[g],
            device_id=(me, base + lax.rem(g + j, H)), device_id_type=MESH,
        )

    answer = zeros
    current = rounded
    rnd = 0
    back = None
    for level in range(LEVELS):
        scatter(rnd, level, False, current, inner(level))
        if rnd == 0:
            sent_row(*before)
            fwd_buf[g] = forward
            for j in range(1, H):
                fwd_copy(j).start()
        if back is not None:
            scattered(*back)
        back = (rnd, level, False)
        solved = reduce(rnd, level, False, rs_src[rnd, me].astype(f32))
        answer = answer + jnp.where(row_level == level, solved, zeros)
        top = highs[level + 1] if level + 1 < LEVELS else -1
        ready = jnp.logical_and(me > top, me <= highs[level])

        @pl.when(jnp.logical_and(giver, ready))
        def _():
            give(answer)

        rnd += 1
        if level + 1 < LEVELS:
            scatter(rnd, level + 1, True, answer.astype(bf16), outer(level + 1))
            scattered(*back)
            back = (rnd, level + 1, True)
            current = (start_value - reduce(rnd, level + 1, True, zeros)).astype(bf16)
            rnd += 1
    scattered(*back)

    for step in range(1, C):
        raw_copy(step).wait_send()
    for j in range(1, H):
        fwd_copy(j).wait_send()
    for j in range(1, H):
        other = lax.rem(g + j, H)
        pltpu.make_async_remote_copy(
            src_ref=fwd_buf.at[g], dst_ref=fwd_buf.at[other],
            send_sem=fwd_send.at[j], recv_sem=fwd_recv.at[other],
            device_id=(me, base + other), device_id_type=MESH,
        ).wait_recv()
    for j in range(H):
        fwd_ref[j * Q:(j + 1) * Q, :] = fwd_buf[j]

    def fin_arrive(s, carry):
        for j in range(H):
            @pl.when(jnp.logical_or(s * C + col != me, g != j))
            def _():
                pltpu.make_async_remote_copy(
                    src_ref=fin_src, dst_ref=fin_buf.at[s, j],
                    send_sem=fin_send.at[0], recv_sem=fin_recv.at[s, j],
                    device_id=(me, col), device_id_type=MESH,
                ).wait_recv()
        return carry

    lax.fori_loop(0, CT, fin_arrive, 0)
    for s in range(CT):
        for j in range(H):
            sol_ref[s, j * Q:(j + 1) * Q, :] = fin_buf[s, j]

    @pl.when(giver)
    def _():
        def one(step, carry):
            fin_copy(lax.rem(me + step, R)).wait_send()
            return carry

        lax.fori_loop(1, R, one, 0)

        @pl.when(jnp.logical_not(local))
        def _():
            fin_copy(me).wait_send()


def finish_kernel(rows_ref, tiles_ref, fwd_ref, sol_ref):
    fwd_ref[:, 0, :] = rows_ref[...]
    for s in range(tiles_ref.shape[0]):
        sol_ref[:, s, :] = tiles_ref[s].astype(jnp.float32)


def shards(R, C, right_sides, factor, node_sizes, row_blocks):
    rhs, row_tiles, T = right_sides.shape
    rows, CT = factor.shape[1], factor.shape[2]
    levels = (node_sizes.shape[0] + 1).bit_length() - 1
    assert row_tiles == 1 and rows == T and CT * C == R
    H = min(C, max(rhs // PACK, 1))
    assert C % H == 0 and rhs % H == 0
    Q = rhs // H
    rounds = 2 * levels - 1
    vmem = pl.BlockSpec(memory_space=pltpu.VMEM)
    smem = pl.BlockSpec(memory_space=pltpu.SMEM)
    dma = pltpu.SemaphoreType.DMA
    bf16, f32 = jnp.bfloat16, jnp.float32
    forward, tiles = pl.pallas_call(
        functools.partial(kernel, R, C, CT, levels, H),
        out_shape=(
            jax.ShapeDtypeStruct((rhs, T), f32),
            jax.ShapeDtypeStruct((CT, rhs, T), bf16),
        ),
        in_specs=[smem, smem, vmem, pl.BlockSpec(memory_space=pl.ANY)],
        out_specs=(vmem, vmem),
        scratch_shapes=[
            pltpu.VMEM((C, rows, CT, T), bf16),
            pltpu.VMEM((T // LANES, CHUNK * CT, LANES), f32),
            pltpu.VMEM((rows, R * T), bf16),
            pltpu.VMEM((rounds, Q, T), bf16),
            pltpu.VMEM((rounds, R, Q, T), bf16),
            pltpu.VMEM((rounds, R, Q, T), bf16),
            pltpu.VMEM((rounds, R, Q, T), bf16),
            pltpu.VMEM((H, Q, T), f32),
            pltpu.VMEM((Q, T), bf16),
            pltpu.VMEM((CT, H, Q, T), bf16),
            dma((rounds, R)),
            dma((rounds, R)),
            dma((rounds, R)),
            dma((rounds, R)),
            dma((H,)),
            dma((H,)),
            dma((R,)),
            dma((CT, H)),
            dma((C,)),
            dma((C,)),
            dma,
        ],
        compiler_params=pltpu.CompilerParams(collective_id=0, has_side_effects=True),
        name="tree_solve",
    )(node_sizes, row_blocks, right_sides, factor)

    return pl.pallas_call(
        finish_kernel,
        out_shape=(
            jax.ShapeDtypeStruct((rhs, 1, T), f32),
            jax.ShapeDtypeStruct((rhs, CT, T), f32),
        ),
        in_specs=[vmem, vmem],
        out_specs=(vmem, vmem),
        name="place",
    )(forward, tiles)


def solution(mesh):
    in_specs = (P(None, None, "prow"), P(None, "prow", None, "pcol"), P(), P())
    out_specs = (P(None, None, "prow"), P(None, None, "pcol"))
    body = functools.partial(shards, mesh.shape["prow"], mesh.shape["pcol"])
    return jax.shard_map(
        body, mesh=mesh, in_specs=in_specs, out_specs=out_specs, check_vma=False
    )
```

time: 66.8 us -> 61.3 us (0.918)
  Pallas kernels: 66 us -> 60.4 us
    pallas_call x1, Pallas kernels: 64.3 us -> 58.7 us  [shards(): pl.pallas_call(functools.partial(kernel, R, C, CT, levels, H), out_shape=...]
where the time goes in v1:
time: 61.3 us; the launch traced here: 61 us
  Pallas kernels  60.4 us (99%)
  between operations  0.64 us (1%)
    pallas_call x1, Pallas kernels, shards(): pl.pallas_call(functools.partial(kernel, R, C, CT, levels, H), out_shape=...  58.7 us
    pallas_call x1, Pallas kernels, shards(): pl.pallas_call(finish_kernel, out_shape=(jax.ShapeDtypeStruct((rhs, 1, T)...  1.72 us

profile of v1, /device:TPU:0, one launch (start us, length us, event | category | flops | bytes accessed | tf_op | source)
XLA Modules:
  0.0 61.0 jit_solution(3689309692491382017)
XLA Ops:
  0.6 58.7 %tree_solve.1 = (f32[32,256]{1,0:T(8,128)}, bf16[8,32,256]{2,1,0:T(8,128)(2,1)}) custom-call(s32[7]{0:T(128)} %sizes_ref.1, s32[7,16]{1,0:T(8,128)} %blocks_ref.1, f32[32,1,256]{2,1,0:T(1,128)} %b_ref.1, bf16[1,256,8,256]{3,2,1,0:T(8,128)(2,1)} %factor_ref.1), custom_call_target="tpu_custom_call" | custom-call | tf_op jit(solution)/shard_map/tree_solve/pallas_call | solution.py:413
  59.3 1.7 %place.1 = (f32[32,1,256]{2,1,0:T(1,128)}, f32[32,8,256]{2,1,0:T(8,128)}) custom-call(f32[32,256]{1,0:T(8,128)} %get-tuple-element.4.rows_ref, bf16[8,32,256]{2,1,0:T(8,128)(2,1)} %get-tuple-element.5.tiles_ref), custom_call_target="tpu_custom_call" | custom-call | tf_op jit(solution)/shard_map/place/pallas_call | solution.py:448

commit v2 on v1

--- a/solution.py
+++ b/solution.py
@@ -11,20 +11,22 @@
 NT_DIMS = (((1,), (1,)), ((), ()))
 NN_DIMS = (((1,), (0,)), ((), ()))
 GATHER = 2
-SPLIT = 2
+SPLIT = 16
 CHUNK = 64
 LANES = 128
 PACK = 16
+GRANT = 32 * 1024 * 1024
 
 
 def kernel(
     R, C, CT, LEVELS, H,
-    sizes_ref, blocks_ref, b_ref, factor_ref,
+    sizes_hbm, blocks_hbm, b_hbm, factor_ref,
     fwd_ref, sol_ref,
+    sizes_ref, blocks_ref, b_ref,
     raw, wide, a_ref,
     ag_src, ag_buf, rs_src, rs_buf, fwd_buf, fin_src, fin_buf,
     ag_send, ag_recv, rs_send, rs_recv,
-    fwd_send, fwd_recv, fin_send, fin_recv, raw_send, raw_recv, load_sem,
+    fwd_send, fwd_recv, fin_send, fin_recv, own_sem, raw_send, raw_recv, load_sem, small_sem,
 ):
     SN = sizes_ref.shape[0]
     me = lax.axis_index("prow")
@@ -44,6 +46,14 @@
         highs.append(R - SN + last)
 
     load = pltpu.make_async_copy(factor_ref.at[0], raw.at[col], load_sem)
+    small = [
+        pltpu.make_async_copy(src, dst, small_sem.at[i])
+        for i, (src, dst) in enumerate(
+            ((sizes_hbm, sizes_ref), (blocks_hbm, blocks_ref), (b_hbm, b_ref))
+        )
+    ]
+    for copy in small:
+        copy.start()
     load.start()
     barrier = pltpu.get_barrier_semaphore()
 
@@ -69,6 +79,8 @@
 
     lax.fori_loop(0, C - H, greet_row, 0)
 
+    for copy in small:
+        copy.wait()
     ends = []
     total = jnp.int32(0)
     for s in range(SN):
@@ -152,10 +164,18 @@
         relayout(origin)
         return carry
 
+    def settle(sem, count, most, sent):
+        for n in range(1, most + 1):
+            done = pltpu.make_async_remote_copy(
+                src_ref=rs_buf.at[0, 0:n], dst_ref=rs_buf.at[0, 0:n],
+                send_sem=sem, recv_sem=sem, device_id=(me, col), device_id_type=MESH,
+            )
+            pl.when(count == n)(done.wait_send if sent else done.wait_recv)
+
     def ag_copy(rnd, k):
         return pltpu.make_async_remote_copy(
             src_ref=ag_src.at[rnd], dst_ref=ag_buf.at[rnd, me],
-            send_sem=ag_send.at[rnd, k], recv_sem=ag_recv.at[rnd, me],
+            send_sem=ag_send.at[rnd], recv_sem=ag_recv.at[rnd, me // GATHER],
             device_id=(k, col), device_id_type=MESH,
         )
 
@@ -179,27 +199,23 @@
 
     def sent_row(rnd, level, far):
         start, stop = forward_range(level, far)
-        lax.fori_loop(start, stop, lambda k, x: (ag_copy(rnd, k).wait_send(), x)[1], 0)
-
-    def row_arrive(rnd, k):
-        pltpu.make_async_remote_copy(
-            src_ref=ag_src.at[rnd], dst_ref=ag_buf.at[rnd, k],
-            send_sem=ag_send.at[rnd, k], recv_sem=ag_recv.at[rnd, k],
-            device_id=(me, col), device_id_type=MESH,
-        ).wait_recv()
+        settle(ag_send.at[rnd], stop - start, R - 1, True)
 
     def multiply(rnd, level, far, masks):
         lo, hi = lows[level], highs[level]
         zero = jnp.zeros((Q, T), bf16)
         out = None
-        for last in range(hi + 1, lo, -GATHER):
-            group = range(max(last - GATHER, lo), last)
-            for k in reversed(group):
-                if far:
-                    due = jnp.logical_and(me > k, me >= lows[level - 1])
-                else:
-                    due = jnp.logical_and(me > k, me <= min(hi, k + widest - 1))
-                pl.when(due)(functools.partial(row_arrive, rnd, k))
+        for part in range(hi // GATHER, lo // GATHER - 1, -1):
+            last = min(part * GATHER + GATHER, hi + 1)
+            group = range(max(part * GATHER, lo), last)
+            if far:
+                first, stop = group[0], jnp.minimum(me, last)
+                due = me >= lows[level - 1]
+            else:
+                first, stop = jnp.maximum(group[0], me - widest + 1), jnp.minimum(me, last)
+                due = me <= hi
+            count = jnp.where(due, jnp.maximum(stop - first, 0), 0)
+            settle(ag_recv.at[rnd, part], count, len(group), False)
             parts = [jnp.where(masks[k], ag_buf[rnd, k], zero) for k in group]
             value = lax.dot_general(
                 jnp.concatenate(parts, axis=1), a_ref[:, group[0] * T:last * T], NT_DIMS,
@@ -237,17 +253,22 @@
     def rs_copy(rnd, t):
         return pltpu.make_async_remote_copy(
             src_ref=rs_src.at[rnd, t], dst_ref=rs_buf.at[rnd, me],
-            send_sem=rs_send.at[rnd, t], recv_sem=rs_recv.at[rnd, me],
+            send_sem=rs_send.at[rnd], recv_sem=rs_recv.at[rnd],
             device_id=(t, col), device_id_type=MESH,
         )
 
-    def goes(level, far, t):
+    def backward_range(level, far):
         if far:
-            return jnp.logical_and(me > t, me >= lows[level - 1])
-        return jnp.logical_and(me > t, me <= min(highs[level], t + widest - 1))
+            first, active = lows[level], me >= lows[level - 1]
+        else:
+            first = jnp.maximum(lows[level], me - widest + 1)
+            active = me <= highs[level]
+        stop = jnp.minimum(me, highs[level] + 1)
+        return first, jnp.where(active, jnp.maximum(stop, first), first)
 
     def scatter(rnd, level, far, value, masks):
         lo, hi = lows[level], highs[level]
+        start, stop = backward_range(level, far)
         for first in range(lo, hi + 1, SPLIT):
             group = range(first, min(first + SPLIT, hi + 1))
             blocks = lax.dot_general(
@@ -258,37 +279,39 @@
                 rs_src[rnd, t] = jnp.where(
                     masks[t], blocks[:, i * T:(i + 1) * T], zeros
                 ).astype(bf16)
-                pl.when(goes(level, far, t))(rs_copy(rnd, t).start)
+            lax.fori_loop(
+                jnp.maximum(start, group[0]), jnp.minimum(stop, group[-1] + 1),
+                lambda t, x: (rs_copy(rnd, t).start(), x)[1], 0,
+            )
 
     def scattered(rnd, level, far):
-        for t in range(lows[level], highs[level] + 1):
-            pl.when(goes(level, far, t))(rs_copy(rnd, t).wait_send)
+        start, stop = backward_range(level, far)
+        settle(rs_send.at[rnd], stop - start, highs[level] + 1 - lows[level], True)
 
     def reduce(rnd, level, far, out):
-        def arrive(k, carry):
-            pltpu.make_async_remote_copy(
-                src_ref=rs_src.at[rnd, 0], dst_ref=rs_buf.at[rnd, k],
-                send_sem=rs_send.at[rnd, 0], recv_sem=rs_recv.at[rnd, k],
-                device_id=(k, col), device_id_type=MESH,
-            ).wait_recv()
-            return carry + rs_buf[rnd, k].astype(f32)
-
-        active = jnp.logical_and(me >= lows[level], me <= highs[level])
+        lo, hi = lows[level], highs[level]
+        active = jnp.logical_and(me >= lo, me <= hi)
         if far:
-            start, last = jnp.maximum(me + 1, lows[level - 1]), jnp.int32(R - 1)
+            first, last = lows[level - 1], R - 1
         else:
-            start = me + 1
-            last = jnp.minimum(me + widest - 1, highs[level])
-        stop = jnp.where(active, jnp.maximum(last + 1, start), start)
-        return lax.fori_loop(start, stop, arrive, out)
+            first, last = lo + 1, hi
+        start = jnp.maximum(me + 1, first)
+        stop = jnp.minimum(me + (R if far else widest - 1), last) + 1
+        stop = jnp.where(active, jnp.maximum(stop, start), start)
+        settle(rs_recv.at[rnd], stop - start, last + 1 - first, False)
+        for k in range(first, last + 1):
+            due = jnp.logical_and(start <= k, k < stop)
+            out = out + jnp.where(due, rs_buf[rnd, k].astype(f32), zeros)
+        return out
 
     def fin_copy(row):
         return pltpu.make_async_remote_copy(
             src_ref=fin_src, dst_ref=fin_buf.at[me // C, g],
-            send_sem=fin_send.at[row], recv_sem=fin_recv.at[me // C, g],
+            send_sem=fin_send, recv_sem=fin_recv,
             device_id=(row, lax.rem(me, C)), device_id_type=MESH,
         )
 
+    own_copy = pltpu.make_async_copy(fin_src, fin_buf.at[me // C, g], own_sem)
     giver = lax.rem(me, C) // H == col // H
     local = lax.rem(me, C) == col
 
@@ -303,7 +326,7 @@
 
         @pl.when(local)
         def _():
-            fin_buf[me // C, g] = value.astype(bf16)
+            own_copy.start()
 
         @pl.when(jnp.logical_not(local))
         def _():
@@ -362,33 +385,15 @@
     for j in range(H):
         fwd_ref[j * Q:(j + 1) * Q, :] = fwd_buf[j]
 
-    def fin_arrive(s, carry):
-        for j in range(H):
-            @pl.when(jnp.logical_or(s * C + col != me, g != j))
-            def _():
-                pltpu.make_async_remote_copy(
-                    src_ref=fin_src, dst_ref=fin_buf.at[s, j],
-                    send_sem=fin_send.at[0], recv_sem=fin_recv.at[s, j],
-                    device_id=(me, col), device_id_type=MESH,
-                ).wait_recv()
-        return carry
-
-    lax.fori_loop(0, CT, fin_arrive, 0)
+    pl.when(local)(own_copy.wait)
+    settle(fin_recv, CT * H - jnp.where(local, 1, 0), CT * H, False)
     for s in range(CT):
         for j in range(H):
             sol_ref[s, j * Q:(j + 1) * Q, :] = fin_buf[s, j]
 
     @pl.when(giver)
     def _():
-        def one(step, carry):
-            fin_copy(lax.rem(me + step, R)).wait_send()
-            return carry
-
-        lax.fori_loop(1, R, one, 0)
-
-        @pl.when(jnp.logical_not(local))
-        def _():
-            fin_copy(me).wait_send()
+        settle(fin_send, R - jnp.where(local, 1, 0), R, True)
 
 
 def finish_kernel(rows_ref, tiles_ref, fwd_ref, sol_ref):
@@ -407,7 +412,6 @@
     Q = rhs // H
     rounds = 2 * levels - 1
     vmem = pl.BlockSpec(memory_space=pltpu.VMEM)
-    smem = pl.BlockSpec(memory_space=pltpu.SMEM)
     dma = pltpu.SemaphoreType.DMA
     bf16, f32 = jnp.bfloat16, jnp.float32
     forward, tiles = pl.pallas_call(
@@ -416,9 +420,12 @@
             jax.ShapeDtypeStruct((rhs, T), f32),
             jax.ShapeDtypeStruct((CT, rhs, T), bf16),
         ),
-        in_specs=[smem, smem, vmem, pl.BlockSpec(memory_space=pl.ANY)],
+        in_specs=[pl.BlockSpec(memory_space=pl.ANY)] * 4,
         out_specs=(vmem, vmem),
         scratch_shapes=[
+            pltpu.SMEM(node_sizes.shape, jnp.int32),
+            pltpu.SMEM(row_blocks.shape, jnp.int32),
+            pltpu.VMEM(right_sides.shape, f32),
             pltpu.VMEM((C, rows, CT, T), bf16),
             pltpu.VMEM((T // LANES, CHUNK * CT, LANES), f32),
             pltpu.VMEM((rows, R * T), bf16),
@@ -429,21 +436,28 @@
             pltpu.VMEM((H, Q, T), f32),
             pltpu.VMEM((Q, T), bf16),
             pltpu.VMEM((CT, H, Q, T), bf16),
-            dma((rounds, R)),
-            dma((rounds, R)),
-            dma((rounds, R)),
-            dma((rounds, R)),
+            dma((rounds,)),
+            dma((rounds, pl.cdiv(R, GATHER))),
+            dma((rounds,)),
+            dma((rounds,)),
             dma((H,)),
             dma((H,)),
-            dma((R,)),
-            dma((CT, H)),
+            dma,
+            dma,
+            dma,
             dma((C,)),
             dma((C,)),
             dma,
+            dma((3,)),
         ],
-        compiler_params=pltpu.CompilerParams(collective_id=0, has_side_effects=True),
+        compiler_params=pltpu.CompilerParams(
+            collective_id=0, has_side_effects=True, vmem_limit_bytes=GRANT
+        ),
         name="tree_solve",
-    )(node_sizes, row_blocks, right_sides, factor)
+    )(*(
+        pltpu.with_memory_space_constraint(x, pltpu.HBM)
+        for x in (node_sizes, row_blocks, right_sides, factor)
+    ))
 
     return pl.pallas_call(
         finish_kernel,
@@ -453,6 +467,7 @@
         ),
         in_specs=[vmem, vmem],
         out_specs=(vmem, vmem),
+        compiler_params=pltpu.CompilerParams(vmem_limit_bytes=GRANT),
         name="place",
     )(forward, tiles)
 

time: 61.3 us -> 55.5 us (0.905)
  Pallas kernels: 60.4 us -> 54.7 us
    pallas_call x1, Pallas kernels: 58.7 us -> 53.9 us  [shards(): pl.pallas_call(functools.partial(kernel, R, C, CT, levels, H), out_shape=...]
    pallas_call x1, Pallas kernels: 1.72 us -> 0.8 us  [shards(): pl.pallas_call(finish_kernel, out_shape=(jax.ShapeDtypeStruct((rhs, 1, T)...]
where the time goes in v2:
time: 55.5 us; the launch traced here: 55.4 us
  Pallas kernels  54.7 us (99%)
  between operations  0.64 us (1%)
    pallas_call x1, Pallas kernels, shards(): pl.pallas_call(functools.partial(kernel, R, C, CT, levels, H), out_shape=...  53.9 us

profile of v2, /device:TPU:0, one launch (start us, length us, event | category | flops | bytes accessed | tf_op | source)
XLA Modules:
  0.0 55.4 jit_solution(17840478040079290146)
XLA Ops:
  0.6 53.9 %tree_solve.1 = (f32[32,256]{1,0:T(8,128)S(1)}, bf16[8,32,256]{2,1,0:T(8,128)(2,1)S(1)}) custom-call(s32[7]{0:T(128)} %sizes_hbm.1, s32[7,16]{1,0:T(8,128)} %blocks_hbm.1, f32[32,1,256]{2,1,0:T(1,128)} %b_hbm.1, bf16[1,256,8,256]{3,2,1,0:T(8,128)(2,1)} %factor_ref.1), custom_call_target="tpu_custom_call" | custom-call | tf_op jit(solution)/shard_map/tree_solve/pallas_call | solution.py:417
  54.6 0.8 %place.1 = (f32[32,1,256]{2,1,0:T(1,128)}, f32[32,8,256]{2,1,0:T(8,128)}) custom-call(f32[32,256]{1,0:T(8,128)S(1)} %get-tuple-element.4.rows_ref, bf16[8,32,256]{2,1,0:T(8,128)(2,1)S(1)} %get-tuple-element.5.tiles_ref), custom_call_target="tpu_custom_call" | custom-call | tf_op jit(solution)/shard_map/place/pallas_call | solution.py:462

commit v3 on v2

--- a/solution.py
+++ b/solution.py
@@ -10,8 +10,8 @@
 MESH = pl.DeviceIdType.MESH
 NT_DIMS = (((1,), (1,)), ((), ()))
 NN_DIMS = (((1,), (0,)), ((), ()))
-GATHER = 2
-SPLIT = 16
+GATHER = 4
+SPLIT = 8
 CHUNK = 64
 LANES = 128
 PACK = 16
@@ -193,7 +193,7 @@
         start, stop = forward_range(level, far)
         ag_src[rnd] = value
         lax.fori_loop(
-            0, stop - start, lambda i, x: (ag_copy(rnd, stop - 1 - i).start(), x)[1], 0
+            0, stop - start, lambda i, x: (ag_copy(rnd, start + i).start(), x)[1], 0
         )
         ag_buf[rnd, me] = value
 
@@ -205,7 +205,7 @@
         lo, hi = lows[level], highs[level]
         zero = jnp.zeros((Q, T), bf16)
         out = None
-        for part in range(hi // GATHER, lo // GATHER - 1, -1):
+        for part in range(lo // GATHER, hi // GATHER + 1):
             last = min(part * GATHER + GATHER, hi + 1)
             group = range(max(part * GATHER, lo), last)
             if far:
@@ -216,12 +216,19 @@
                 due = me <= hi
             count = jnp.where(due, jnp.maximum(stop - first, 0), 0)
             settle(ag_recv.at[rnd, part], count, len(group), False)
-            parts = [jnp.where(masks[k], ag_buf[rnd, k], zero) for k in group]
-            value = lax.dot_general(
-                jnp.concatenate(parts, axis=1), a_ref[:, group[0] * T:last * T], NT_DIMS,
-                preferred_element_type=f32,
-            )
-            out = value if out is None else out + value
+
+            def add(acc, group=group):
+                parts = [jnp.where(masks[k], ag_buf[rnd, k], zero) for k in group]
+                return acc + lax.dot_general(
+                    jnp.concatenate(parts, axis=1),
+                    a_ref[:, group[0] * T:(group[-1] + 1) * T], NT_DIMS,
+                    preferred_element_type=f32,
+                )
+
+            if out is None:
+                out = add(jnp.zeros((Q, T), f32))
+            else:
+                out = lax.cond(group[0] <= me, add, lambda acc: acc, out)
         return out
 
     forward = zeros
@@ -269,19 +276,23 @@
     def scatter(rnd, level, far, value, masks):
         lo, hi = lows[level], highs[level]
         start, stop = backward_range(level, far)
-        for first in range(lo, hi + 1, SPLIT):
-            group = range(first, min(first + SPLIT, hi + 1))
-            blocks = lax.dot_general(
-                value, a_ref[:, group[0] * T:(group[-1] + 1) * T], NN_DIMS,
-                preferred_element_type=f32,
-            )
-            for i, t in enumerate(group):
-                rs_src[rnd, t] = jnp.where(
-                    masks[t], blocks[:, i * T:(i + 1) * T], zeros
-                ).astype(bf16)
+        for part in range(hi // SPLIT, lo // SPLIT - 1, -1):
+            group = range(max(part * SPLIT, lo), min(part * SPLIT + SPLIT, hi + 1))
+
+            @pl.when(group[0] <= me)
+            def _(group=group):
+                blocks = lax.dot_general(
+                    value, a_ref[:, group[0] * T:(group[-1] + 1) * T], NN_DIMS,
+                    preferred_element_type=f32,
+                )
+                for i, t in enumerate(group):
+                    rs_src[rnd, t] = jnp.where(
+                        masks[t], blocks[:, i * T:(i + 1) * T], zeros
+                    ).astype(bf16)
+
             lax.fori_loop(
                 jnp.maximum(start, group[0]), jnp.minimum(stop, group[-1] + 1),
-                lambda t, x: (rs_copy(rnd, t).start(), x)[1], 0,
+                lambda t, x, a=group[0], z=group[-1] + 1: (rs_copy(rnd, jnp.maximum(start, a) + jnp.minimum(stop, z) - 1 - t).start(), x)[1], 0,
             )
 
     def scattered(rnd, level, far):

time: 55.5 us -> 52 us (0.937)
  Pallas kernels: 54.7 us -> 51.3 us
    pallas_call x1, Pallas kernels: 53.9 us -> 50.5 us  [shards(): pl.pallas_call(functools.partial(kernel, R, C, CT, levels, H), out_shape=...]
where the time goes in v3:
time: 52 us; the launch traced here: 51.9 us
  Pallas kernels  51.3 us (99%)
  between operations  0.64 us (1%)
    pallas_call x1, Pallas kernels, shards(): pl.pallas_call(functools.partial(kernel, R, C, CT, levels, H), out_shape=...  50.5 us

profile of v3, /device:TPU:0, one launch (start us, length us, event | category | flops | bytes accessed | tf_op | source)
XLA Modules:
  0.0 51.9 jit_solution(3387172883997153440)
XLA Ops:
  0.6 50.5 %tree_solve.1 = (f32[32,256]{1,0:T(8,128)S(1)}, bf16[8,32,256]{2,1,0:T(8,128)(2,1)S(1)}) custom-call(s32[7]{0:T(128)} %sizes_hbm.1, s32[7,16]{1,0:T(8,128)} %blocks_hbm.1, f32[32,1,256]{2,1,0:T(1,128)} %b_hbm.1, bf16[1,256,8,256]{3,2,1,0:T(8,128)(2,1)} %factor_ref.1), custom_call_target="tpu_custom_call" | custom-call | tf_op jit(solution)/shard_map/tree_solve/pallas_call | solution.py:428
  51.1 0.8 %place.1 = (f32[32,1,256]{2,1,0:T(1,128)}, f32[32,8,256]{2,1,0:T(8,128)}) custom-call(f32[32,256]{1,0:T(8,128)S(1)} %get-tuple-element.4.rows_ref, bf16[8,32,256]{2,1,0:T(8,128)(2,1)S(1)} %get-tuple-element.5.tiles_ref), custom_call_target="tpu_custom_call" | custom-call | tf_op jit(solution)/shard_map/place/pallas_call | solution.py:473
